TPU v7x, 32 devices: a whole 2x2x4 slice. The times are simulated.
32 devices in a mesh: row: 8 (over y, x, core), col: 4 (over z).
Axes of the slice: x: 2, y: 2, z: 4, core: 2. Of those that a mesh axis runs over, the one named last changes fastest.
Arguments:
- layer_input: bfloat16 [256, 6144], P('row', 'col'), may hold values from -6 to 6
- norm_gain_rows: float32 [2, 6144], P(None, 'col'), may hold values from 0.1 to 1.9
- norm_bias_rows: float32 [2, 6144], P(None, 'col'), may hold values from -3 to 3
- query_key_value_weight: bfloat16 [6144, 3, 6144], P('col', None, 'row'), may hold values from -0.078125 to 0.078125
- adapter_down_maps: bfloat16 [64, 16, 6144], P(None, None, 'col'), may hold values from -0.078125 to 0.078125
- adapter_up_maps: bfloat16 [64, 16, 3, 6144], P(None, None, None, 'row'), may hold values from -6.5 to 6.5
- output_projection: bfloat16 [6144, 6144], P('row', 'col'), may hold values from -0.078125 to 0.078125
- up_projection: bfloat16 [6144, 24576], P('col', 'row'), may hold values from -0.078125 to 0.078125
- down_projection: bfloat16 [24576, 6144], P('row', 'col'), may hold values from -0.0390625 to 0.0390625
- prompt_token_length: int32 [4], replicated, may hold values from 1 to 64, 160 in all
- adapter_index: int32 [4], replicated, may hold values from 0 to 63
- prompt_page_map: int32 [4], replicated, may hold values from 0 to 3, each once
Outputs:
- new_hidden: bfloat16 [256, 6144], P('row', 'col')
- kv_pages: bfloat16 [4, 2, 64, 6144], P('col', None, None, 'row')
Inputs may be any that keep to these rules, and one draw needn't show every extreme that they name: `prompt_page_map`: each page is named by exactly one prompt. `prompt_token_length`: the prompts together hold 4 * 64 * 5 // 8 real tokens; some prompt fills all 64 positions.
All inputs are finite; a program needn't handle non-finite values.
Results may differ from a plain program's by a relative error of at most 0.023.
Values may be sent and summed in bfloat16 or wider, within the bound.
A program may use at most 128 MiB of HBM per device.

v0:
```python
import jax
import jax.numpy as jnp
from jax import lax
from jax.sharding import PartitionSpec as P

MODEL_WIDTH = 6144
HD = 96
ROT = 24


def normalize(hidden_f32, moments, gain_row, bias_row):
    row_mean = (moments[0] / MODEL_WIDTH)[:, None]
    row_var = (moments[1] / MODEL_WIDTH)[:, None] - row_mean * row_mean
    return ((hidden_f32 - row_mean) * lax.rsqrt(row_var + 1e-05) * gain_row + bias_row).astype(
        jnp.bfloat16
    )


def rotate(heads_in, positions):
    half_rot = ROT // 2
    inv_freq = 10000.0 ** (-jnp.arange(half_rot, dtype=jnp.float32) * 2.0 / ROT)
    angles = positions.astype(jnp.float32)[:, None] * inv_freq[None, :]
    cosine = jnp.cos(angles)[:, None, :]
    sine_part = jnp.sin(angles)[:, None, :]
    front_part = heads_in[..., :half_rot]
    back_part = heads_in[..., half_rot:ROT]
    return jnp.concatenate(
        [
            front_part * cosine - back_part * sine_part,
            back_part * cosine + front_part * sine_part,
            heads_in[..., ROT:],
        ],
        axis=-1,
    )


def per_device(
    layer_input,
    norm_gain_rows,
    norm_bias_rows,
    query_key_value_weight,
    adapter_down_maps,
    adapter_up_maps,
    output_projection,
    up_projection,
    down_projection,
    prompt_token_length,
    adapter_index,
    prompt_page_map,
):
    col_width = layer_input.shape[1]
    hidden_f32 = layer_input.astype(jnp.float32)
    moments = lax.psum(
        (jnp.sum(hidden_f32, axis=-1), jnp.sum(hidden_f32 * hidden_f32, axis=-1)), "col"
    )
    normed_attn = normalize(hidden_f32, moments, norm_gain_rows[0], norm_bias_rows[0])
    normed_mlp = normalize(hidden_f32, moments, norm_gain_rows[1], norm_bias_rows[1])
    normed_attn, normed_mlp = (
        lax.all_gather(normed_attn, "row", axis=0, tiled=True),
        lax.all_gather(normed_mlp, "row", axis=0, tiled=True),
    )
    col_count = lax.axis_size("col")
    prompt_span = normed_attn.shape[0] // col_count
    wide_weight = query_key_value_weight.reshape(col_width, -1)
    query_key_value_width = wide_weight.shape[1]
    adapter_wide_term = adapter_up_maps.reshape(
        adapter_up_maps.shape[0], adapter_up_maps.shape[1], query_key_value_width
    )
    slot_index = jnp.arange(col_count, dtype=jnp.int32)
    token_blocks = normed_attn.reshape(col_count, prompt_span, col_width)
    prompt = lax.axis_index("col")
    tok_slice = token_blocks.reshape(lax.axis_size("col") * prompt_span, col_width)
    base_term = jnp.dot(tok_slice, wide_weight, preferred_element_type=jnp.float32)
    selected_adapter = jnp.take(adapter_index, slot_index, axis=0)
    select_down = adapter_down_maps[selected_adapter]
    select_up = adapter_wide_term[selected_adapter]
    low_rank = jnp.einsum(
        "pld,prd->plr", token_blocks, select_down, preferred_element_type=jnp.float32
    ).astype(jnp.bfloat16)
    extra_term = jnp.einsum("plr,prk->plk", low_rank, select_up, preferred_element_type=jnp.float32)
    qkv_rows = lax.psum_scatter(
        (
            base_term
            + extra_term.reshape(lax.axis_size("col") * prompt_span, query_key_value_width)
        ).astype(jnp.bfloat16),
        "col",
        scatter_dimension=0,
        tiled=True,
    ).astype(jnp.float32)
    local_heads = query_key_value_width // (3 * HD)
    qkv_rows = qkv_rows.reshape(prompt_span, 3, local_heads, HD)
    positions = jnp.arange(prompt_span, dtype=jnp.int32)
    prompt_len = lax.dynamic_slice_in_dim(prompt_token_length, prompt, 1, 0)[0]
    live_mask = positions < prompt_len
    query = rotate(qkv_rows[:, 0], positions).astype(jnp.bfloat16)
    key_rows = rotate(qkv_rows[:, 1], positions).astype(jnp.bfloat16)
    value_rows = qkv_rows[:, 2].astype(jnp.bfloat16)
    zero_key = jnp.zeros_like(key_rows)
    key_rows = jnp.where(live_mask[:, None, None], key_rows, zero_key)
    value_rows = jnp.where(live_mask[:, None, None], value_rows, zero_key)
    scores = jnp.einsum(
        "qhe,khe->hqk", query, key_rows, preferred_element_type=jnp.float32
    ) / jnp.sqrt(jnp.float32(HD))
    allowed = (positions[None, :] <= positions[:, None]) & live_mask[None, :]
    scores = jnp.where(allowed[None, :, :], scores, jnp.float32(-1e30))
    top_score = jnp.max(scores, axis=-1, keepdims=True)
    expo = jnp.exp(scores - top_score)
    probs = (expo / jnp.sum(expo, axis=-1, keepdims=True)).astype(jnp.bfloat16)
    attended = jnp.einsum(
        "hqk,khe->qhe", probs, value_rows, preferred_element_type=jnp.float32
    ).astype(jnp.bfloat16)
    attended = attended.reshape(prompt_span, local_heads * HD)
    page_local = jnp.stack(
        [key_rows.reshape(prompt_span, -1), value_rows.reshape(prompt_span, -1)], axis=0
    )[None]
    target_hit = (prompt_page_map == prompt).astype(jnp.bfloat16)
    kv_pages = jnp.einsum(
        "p,pslk->slk",
        target_hit,
        lax.all_gather(page_local, "col", axis=0, tiled=True),
        preferred_element_type=jnp.float32,
    )[None].astype(jnp.bfloat16)
    tok_slice = normed_mlp
    up_rows = lax.psum_scatter(
        jnp.dot(tok_slice, up_projection, preferred_element_type=jnp.float32).astype(jnp.bfloat16),
        "col",
        scatter_dimension=0,
        tiled=True,
    ).astype(jnp.float32)
    hidden = jax.nn.gelu(up_rows, approximate=False).astype(jnp.bfloat16)
    attn_whole, hidden_whole = (
        lax.all_gather(attended, "col", axis=0, tiled=True),
        lax.all_gather(hidden, "col", axis=0, tiled=True),
    )
    branch = lax.psum_scatter(
        (
            jnp.dot(attn_whole, output_projection, preferred_element_type=jnp.float32)
            + jnp.dot(hidden_whole, down_projection, preferred_element_type=jnp.float32)
        ).astype(jnp.bfloat16),
        "row",
        scatter_dimension=0,
        tiled=True,
    ).astype(jnp.float32)
    new_hidden = (layer_input.astype(jnp.float32) + branch).astype(jnp.bfloat16)
    return (new_hidden, kv_pages)


def solution(mesh):
    return jax.shard_map(
        per_device,
        mesh=mesh,
        in_specs=(
            P("row", "col"),
            P(None, "col"),
            P(None, "col"),
            P("col", None, "row"),
            P(None, None, "col"),
            P(None, None, None, "row"),
            P("row", "col"),
            P("col", "row"),
            P("row", "col"),
            P(),
            P(),
            P(),
        ),
        out_specs=(P("row", "col"), P("col", None, None, "row")),
        check_vma=False,
    )
```

profile of v0, /device:TPU:0, one launch (start us, length us, event | category | flops | bytes accessed | tf_op | source)
XLA Modules:
  0.0 197.1 jit_solution(14919838215069900529)
XLA Ops:
  7.2 1.2 convert_reduce_fusion
  8.4 13.5 %all-reduce = (f32[32]{0:T(128)S(1)}, f32[32]{0:T(128)S(1)}) all-reduce(f32[32]{0:T(128)S(1)} %get-tuple-element.3, f32[32]{0:T(128)S(1)} %get-tuple-element.2), channel_id=1, replica_groups=mesh['row'=8,'col'=4] {'col'}, use_global_device_ids=true, to_apply=%region_3.0 | all-reduce | flops 64 | bytes 512 | tf_op jit(solution)/shard_map/psum | solution.py:53
  21.9 0.9 slice_reduce_fusion.2
  22.7 1.0 fusion.45
  23.8 10.4 %all_gather.17 = bf16[256,1536]{1,0:T(8,128)(2,1)S(1)} all-gather(bf16[32,1536]{1,0:T(8,128)(2,1)S(1)} %get-tuple-element.17), channel_id=1, replica_groups=mesh['row'=8,'col'=4] {'row'}, dimensions={0}, use_global_device_ids=true | all-gather | bytes 884736 | tf_op jit(solution)/shard_map/all_gather | solution.py:60
  34.2 7.4 %convolution_convert_fusion = bf16[256,3072]{1,0:T(8,128)(2,1)} fusion(bf16[256,1536]{1,0:T(8,128)(2,1)S(1)} %all_gather.17, bf16[1536,3072]{1,0:T(8,128)(2,1)} %param.19), kind=kOutput, calls=%fused_computation.6 | convolution fusion | flops 2416705536 | bytes 11796480 | tf_op jit(solution)/shard_map/dot_general | solution.py:125
  41.7 4.8 %copy.43 = bf16[64,3,2,8,768]{4,3,1,2,0:T(8,128)(2,1)} copy(bf16[64,3,2,8,768]{4,3,2,1,0:T(8,128)(2,1)} %bitcast.55) | data formatting | bytes 9437184 | tf_op jit(solution)/shard_map/reshape | solution.py:66
  46.5 0.6 gather_fusion
  47.1 2.9 %gather_fusion.2 = bf16[4,16,2304]{2,1,0:T(8,128)(2,1)S(1)} fusion(bf16[64,16,2304]{2,1,0:T(8,128)(2,1)} %bitcast.54, s32[1024]{0:T(1024)S(1)} %pad_clamp_fusion), kind=kCustom, calls=%fused_computation.2 | custom fusion | bytes 589840 | tf_op jit(solution)/shard_map/gather | solution.py:76
  50.0 1.2 gather_fusion.1
  51.3 10.3 %copy.27 = bf16[1536,3,768]{0,2,1:T(8,128)(2,1)} copy(bf16[1536,3,768]{2,0,1:T(8,128)(2,1)} %param.15) | data formatting | bytes 14155776 | tf_op args[3]
  61.6 10.4 %all_gather.15 = bf16[256,1536]{1,0:T(8,128)(2,1)S(1)} all-gather(bf16[32,1536]{1,0:T(8,128)(2,1)S(1)} %get-tuple-element.16), channel_id=1, replica_groups=mesh['row'=8,'col'=4] {'row'}, dimensions={0}, use_global_device_ids=true | all-gather | bytes 884736 | tf_op jit(solution)/shard_map/all_gather | solution.py:59
  72.0 1.7 fusion.7
  73.6 6.2 %fusion.1 = bf16[256,2304]{1,0:T(8,128)(2,1)} fusion(f32[256,2304]{1,0:T(8,128)S(1)} %bitcast.61, bf16[256,1536]{1,0:T(8,128)(2,1)S(1)} %all_gather.15, bf16[1536,2304]{0,1:T(8,128)(2,1)} %bitcast.53), kind=kOutput, calls=%fused_computation.5 | convolution fusion | flops 1813118976 | bytes 11403264 | tf_op jit(solution)/shard_map/dot_general | solution.py:73
  79.9 0.6 dynamic_slice.3
  80.5 3.4 %fusion.9 = bf16[64,3072]{1,0:T(8,128)(2,1)} fusion(bf16[64,3072]{1,0:T(8,128)(2,1)} %reduce-scatter.6.cloned.1.call-done), kind=kLoop, calls=%fused_computation.21 | loop fusion | flops 12976128 | bytes 786432 | tf_op jit(solution)/shard_map/convert_element_type | solution.py:130
  84.0 0.7 iota_compare_fusion.1
  84.9 21.5 %reduce-scatter.4.cloned.1.call-done = bf16[64,2304]{1,0:T(8,128)(2,1)} async-done(((bf16[256,2304]{1,0:T(8,128)(2,1)}), bf16[64,2304]{1,0:T(8,128)(2,1)}) %reduce-scatter.4.cloned.1.call-update) | async-done | bytes 294928 | tf_op jit(solution)/shard_map/reduce_scatter | solution.py:81
  106.4 1.5 reshape.213
  108.8 0.3 fusion.80
  109.1 0.3 fusion.4
  109.9 17.8 %all_gather.16 = bf16[256,768]{1,0:T(8,128)(2,1)S(1)} all-gather(bf16[64,768]{1,0:T(8,128)(2,1)S(1)} %reshape.211), channel_id=1, replica_groups=mesh['row'=8,'col'=4] {'col'}, dimensions={0}, use_global_device_ids=true | all-gather | bytes 491520 | tf_op jit(solution)/shard_map/all_gather | solution.py:132
  127.8 19.5 %all-gather.3.cloned.1.call-done = bf16[256,3072]{1,0:T(8,128)(2,1)} async-done(((bf16[64,3072]{1,0:T(8,128)(2,1)}), bf16[256,3072]{1,0:T(8,128)(2,1)}) %all-gather.3.cloned.1.call-update) | async-done | bytes 1572880 | tf_op jit(solution)/shard_map/all_gather | solution.py:133
  147.2 5.6 %fusion.86 = f32[256,1536]{1,0:T(8,128)S(1)} fusion(bf16[256,3072]{1,0:T(8,128)(2,1)} %all-gather.3.cloned.1.call-done, bf16[3072,1536]{1,0:T(8,128)(2,1)} %param.20), kind=kOutput, calls=%fused_computation.124 | convolution fusion | flops 2415919104 | bytes 12582912 | tf_op jit(solution)/shard_map/dot_general | solution.py:138
  152.9 1.7 fusion.2
  154.7 0.8 convert_element_type.121
  155.7 1.1 broadcast_select_fusion.1
  156.9 18.0 %all-gather = bf16[8,64,768]{2,1,0:T(8,128)(2,1)S(1)} all-gather(bf16[2,64,768]{2,1,0:T(8,128)(2,1)S(1)} %pad_maximum_fusion), channel_id=2, replica_groups=mesh['row'=8,'col'=4] {'col'}, dimensions={0}, use_global_device_ids=true | all-gather | bytes 983040 | tf_op jit(solution)/shard_map/all_gather | solution.py:120
  175.0 0.7 fusion.39
  175.7 0.7 copy.59
  176.4 12.7 %reduce-scatter.8.cloned.1.call-done = bf16[32,1536]{1,0:T(8,128)(2,1)} async-done(((bf16[256,1536]{1,0:T(8,128)(2,1)}), bf16[32,1536]{1,0:T(8,128)(2,1)}) %reduce-scatter.8.cloned.1.call-update) | async-done | bytes 98320 | tf_op jit(solution)/shard_map/reduce_scatter | solution.py:135
  189.1 1.6 fusion.49
  (49 shorter events, 2.2 us)
Async XLA Ops:
  7.2 42.9 %copy-start = (bf16[64,16,1536]{2,1,0:T(8,128)(2,1)S(1)}, bf16[64,16,1536]{2,1,0:T(8,128)(2,1)}, u32[]{:S(2)}) copy-start(bf16[64,16,1536]{2,1,0:T(8,128)(2,1)} %param.16) | copy-start | bytes 9437188
  7.2 73.3 %reduce-scatter.6.cloned.1.call-start = ((), (), s32[]{:S(2)}) async-start(), calls=%async_computation.4 | async-start | bytes 1966080 | tf_op jit(solution)/shard_map/reduce_scatter | solution.py:124
  41.6 64.8 %reduce-scatter.4.cloned.1.call-start = ((), (), s32[]{:S(2)}) async-start(), calls=%async_computation.3 | async-start | bytes 1474560 | tf_op jit(solution)/shard_map/reduce_scatter | solution.py:81
  41.7 4.8 %copy-start.2 = (s32[4]{0:T(128)S(1)}, s32[4]{0:T(128)}, u32[]{:S(2)}) copy-start(s32[4]{0:T(128)} %param.22) | copy-start | bytes 52
  73.6 6.3 %copy-start.5 = (s32[4]{0:T(128)S(1)}, s32[4]{0:T(128)}, u32[]{:S(2)}) copy-start(s32[4]{0:T(128)} %param.21) | copy-start | bytes 52
  79.8 67.4 %all-gather.3.cloned.1.call-start = ((), (), s32[]{:S(2)}) async-start(), calls=%async_computation.5 | async-start | bytes 1966080 | tf_op jit(solution)/shard_map/all_gather | solution.py:133
  83.9 105.1 %reduce-scatter.8.cloned.1.call-start = ((), (), s32[]{:S(2)}) async-start(), calls=%async_computation.6 | async-start | bytes 884736 | tf_op jit(solution)/shard_map/reduce_scatter | solution.py:135
  127.8 25.1 %copy-start.3 = (bf16[768,1536]{1,0:T(8,128)(2,1)S(1)}, bf16[768,1536]{1,0:T(8,128)(2,1)}, u32[]{:S(2)}) copy-start(bf16[768,1536]{1,0:T(8,128)(2,1)} %param.18) | copy-start | bytes 7077892
  154.6 20.4 %copy-start.6 = (s32[4]{0:T(128)S(1)}, s32[4]{0:T(128)}, u32[]{:S(2)}) copy-start(s32[4]{0:T(128)} %param.23) | copy-start | bytes 52
  155.5 33.5 %copy-start.4 = (bf16[32,1536]{1,0:T(8,128)(2,1)S(1)}, bf16[32,1536]{1,0:T(8,128)(2,1)}, u32[]{:S(2)}) copy-start(bf16[32,1536]{1,0:T(8,128)(2,1)} %param.12) | copy-start | bytes 294916
  155.5 35.1 %copy-start.1 = (bf16[64,16,1536]{2,1,0:T(8,128)(2,1)S(1)}, bf16[64,16,1536]{2,1,0:T(8,128)(2,1)}, u32[]{:S(2)}) copy-start(bf16[64,16,1536]{2,1,0:T(8,128)(2,1)} %param.16) | copy-start | bytes 9437188
Sparse Core Ops, SparseCore 0:
  41.7 32.5 reduce-scatter.5
  79.9 26.4 reduce-scatter.3
  108.0 39.1 all-gather.2
  154.7 34.2 reduce-scatter.7
where the time goes:
time: 198 us; the launch traced here: 197 us
  blocking collectives  70.1 us (35%)
  waiting for transfers between devices  53.7 us (27%)
  local copies, waits for them, and re-layouts  25.3 us (13%)
  matrix products  24.1 us (12%)
  between operations  14 us (7%)
  other arithmetic  9.75 us (5%)
    reduce_scatter x1, waiting for transfers between devices, per_device(): lax.psum_scatter((base_term + extra_term.reshape(lax.axis_size('col') * p...  21.5 us
    all_gather x1, waiting for transfers between devices, per_device(): lax.all_gather(hidden, 'col', axis=0, tiled=True)  19.5 us
    all_gather x1, blocking collectives, per_device(): lax.all_gather(page_local, 'col', axis=0, tiled=True)  18 us
    all_gather x1, blocking collectives, per_device(): lax.all_gather(attended, 'col', axis=0, tiled=True)  17.8 us
    psum x1, blocking collectives, per_device(): lax.psum((jnp.sum(hidden_f32, axis=-1), jnp.sum(hidden_f32 * hidden_f32,...  13.5 us
    reduce_scatter x1, waiting for transfers between devices, per_device(): lax.psum_scatter((jnp.dot(attn_whole, output_projection, preferred_elemen...  12.7 us
    unnamed x18, local copies, waits for them, and re-layouts  10.5 us
    all_gather x1, blocking collectives, per_device(): lax.all_gather(normed_mlp, 'row', axis=0, tiled=True)  10.4 us
  transfers between devices with their start and end apart: 4, of which 3 were waited for; matrix products, arithmetic and copies ran while one was open for 20% of the time, Pallas kernels for 0%

commit v1 on v0

--- a/solution.py
+++ b/solution.py
@@ -6,6 +6,29 @@
 MODEL_WIDTH = 6144
 HD = 96
 ROT = 24
+
+
+def laid_out(blocks, dim):
+    shape = list(blocks.shape[1:])
+    shape[dim] *= blocks.shape[0]
+    return jnp.moveaxis(blocks, 0, dim).reshape(shape)
+
+
+def grow_blocks(x, axis):
+    count, index = (lax.axis_size(axis), lax.axis_index(axis))
+    blocks, stride = (x[None], 1)
+    while stride < count:
+        partner_block = lax.ppermute(blocks, axis, [(i, i ^ stride) for i in range(count)])
+        low = index & stride == 0
+        blocks = jnp.concatenate(
+            [jnp.where(low, blocks, partner_block), jnp.where(low, partner_block, blocks)]
+        )
+        stride *= 2
+    return blocks
+
+
+def collect(value, axis, dim):
+    return laid_out(grow_blocks(value, axis), dim)
 
 
 def normalize(hidden_f32, moments, gain_row, bias_row):
@@ -129,7 +152,7 @@
     ).astype(jnp.float32)
     hidden = jax.nn.gelu(up_rows, approximate=False).astype(jnp.bfloat16)
     attn_whole, hidden_whole = (
-        lax.all_gather(attended, "col", axis=0, tiled=True),
+        collect(attended, "col", 0),
         lax.all_gather(hidden, "col", axis=0, tiled=True),
     )
     branch = lax.psum_scatter(

time: 198 us -> 224 us (1.13)
  waiting for transfers between devices: 53.7 us -> 93.6 us
  blocking collectives: 70.1 us -> 53.2 us
    reduce_scatter x1, waiting for transfers between devices: 0.01 us -> 34.8 us  [per_device(): lax.psum_scatter(jnp.dot(tok_slice, up_projection, preferred_element_type...]
    ppermute x0 -> x2, waiting for transfers between devices: none -> 24.8 us  [grow_blocks(): lax.ppermute(blocks, axis, [(i, i ^ stride) for i in range(count)])]
    all_gather x1 -> x0, blocking collectives: 17.8 us -> none  [per_device(): lax.all_gather(attended, 'col', axis=0, tiled=True)]
    reduce_scatter x1, waiting for transfers between devices: 21.5 us -> 7.15 us  [per_device(): lax.psum_scatter((base_term + extra_term.reshape(lax.axis_size('col') * p...]
    all_gather x1, waiting for transfers between devices: 19.5 us -> 14 us  [per_device(): lax.all_gather(hidden, 'col', axis=0, tiled=True)]
  transfers between devices with their start and end apart: 4 -> 6, of which waited for: 3 -> 6; matrix products, arithmetic and copies ran while one was open for 20% -> 7% of each run, Pallas kernels for 0% -> 0%
where the time goes in v1:
time: 224 us; the launch traced here: 223 us
  waiting for transfers between devices  93.6 us (42%)
  blocking collectives  53.2 us (24%)
  local copies, waits for them, and re-layouts  26 us (12%)
  matrix products  24 us (11%)
  between operations  14 us (6%)
  other arithmetic  9.89 us (4%)
  starting transfers between devices  2.24 us (1%)
    reduce_scatter x1, waiting for transfers between devices, per_device(): lax.psum_scatter(jnp.dot(tok_slice, up_projection, preferred_element_type...  34.8 us
    ppermute x2, waiting for transfers between devices, grow_blocks(): lax.ppermute(blocks, axis, [(i, i ^ stride) for i in range(count)])  24.8 us
    all_gather x1, blocking collectives, per_device(): lax.all_gather(page_local, 'col', axis=0, tiled=True)  18 us
    all_gather x1, waiting for transfers between devices, per_device(): lax.all_gather(hidden, 'col', axis=0, tiled=True)  14 us
    psum x1, blocking collectives, per_device(): lax.psum((jnp.sum(hidden_f32, axis=-1), jnp.sum(hidden_f32 * hidden_f32,...  13.5 us
    reduce_scatter x1, waiting for transfers between devices, per_device(): lax.psum_scatter((jnp.dot(attn_whole, output_projection, preferred_elemen...  12.8 us
    all_gather x1, blocking collectives, per_device(): lax.all_gather(normed_attn, 'row', axis=0, tiled=True)  11.5 us
    unnamed x18, local copies, waits for them, and re-layouts  10.5 us
  transfers between devices with their start and end apart: 6, of which 6 were waited for; matrix products, arithmetic and copies ran while one was open for 7% of the time, Pallas kernels for 0%

profile of v1, /device:TPU:0, one launch (start us, length us, event | category | flops | bytes accessed | tf_op | source)
XLA Modules:
  0.0 223.0 jit_solution(9020402217835824067)
XLA Ops:
  7.2 1.2 convert_reduce_fusion
  8.4 13.5 %all-reduce = (f32[32]{0:T(128)S(1)}, f32[32]{0:T(128)S(1)}) all-reduce(f32[32]{0:T(128)S(1)} %get-tuple-element.3, f32[32]{0:T(128)S(1)} %get-tuple-element.2), channel_id=1, replica_groups=mesh['row'=8,'col'=4] {'col'}, use_global_device_ids=true, to_apply=%region_3.0 | all-reduce | flops 64 | bytes 512 | tf_op jit(solution)/shard_map/psum | solution.py:76
  21.9 0.9 slice_reduce_fusion.2
  22.7 1.0 fusion.45
  23.8 11.5 %all_gather.12 = bf16[256,1536]{1,0:T(8,128)(2,1)} all-gather(bf16[32,1536]{1,0:T(8,128)(2,1)S(1)} %get-tuple-element.20), channel_id=1, replica_groups=mesh['row'=8,'col'=4] {'row'}, dimensions={0}, use_global_device_ids=true | all-gather | bytes 884736 | tf_op jit(solution)/shard_map/all_gather | solution.py:82
  35.2 1.3 gather_fusion
  36.5 4.8 %copy.43 = bf16[64,3,2,8,768]{4,3,1,2,0:T(8,128)(2,1)} copy(bf16[64,3,2,8,768]{4,3,2,1,0:T(8,128)(2,1)} %bitcast.56) | data formatting | bytes 9437184 | tf_op jit(solution)/shard_map/reshape | solution.py:89
  41.3 2.9 %gather_fusion.2 = bf16[4,16,2304]{2,1,0:T(8,128)(2,1)S(1)} fusion(bf16[64,16,2304]{2,1,0:T(8,128)(2,1)} %bitcast.55, s32[1024]{0:T(1024)S(1)} %pad_clamp_fusion), kind=kCustom, calls=%fused_computation.2 | custom fusion | bytes 589840 | tf_op jit(solution)/shard_map/gather | solution.py:99
  44.2 1.2 gather_fusion.1
  45.5 10.3 %copy.27 = bf16[1536,3,768]{0,2,1:T(8,128)(2,1)} copy(bf16[1536,3,768]{2,0,1:T(8,128)(2,1)} %param.15) | data formatting | bytes 14155776 | tf_op args[3]
  55.8 1.6 fusion.7
  57.5 6.0 %fusion.1 = bf16[256,2304]{1,0:T(8,128)(2,1)} fusion(f32[256,2304]{1,0:T(8,128)S(1)} %bitcast.62, bf16[256,1536]{1,0:T(8,128)(2,1)S(1)} %copy-done.2, bf16[1536,2304]{0,1:T(8,128)(2,1)} %bitcast.54), kind=kOutput, calls=%fused_computation.5 | convolution fusion | flops 1813118976 | bytes 11403264 | tf_op jit(solution)/shard_map/dot_general | solution.py:96
  63.6 10.3 %all_gather.13 = bf16[256,1536]{1,0:T(8,128)(2,1)S(1)} all-gather(bf16[32,1536]{1,0:T(8,128)(2,1)S(1)} %get-tuple-element.21), channel_id=1, replica_groups=mesh['row'=8,'col'=4] {'row'}, dimensions={0}, use_global_device_ids=true | all-gather | bytes 884736 | tf_op jit(solution)/shard_map/all_gather | solution.py:83
  73.9 7.5 %convolution_convert_fusion = bf16[256,3072]{1,0:T(8,128)(2,1)} fusion(bf16[256,1536]{1,0:T(8,128)(2,1)S(1)} %all_gather.13, bf16[1536,3072]{1,0:T(8,128)(2,1)} %param.19), kind=kOutput, calls=%fused_computation.6 | convolution fusion | flops 2416705536 | bytes 11796480 | tf_op jit(solution)/shard_map/dot_general | solution.py:148
  82.0 0.7 iota_compare_fusion.1
  83.0 7.1 %reduce-scatter.4.cloned.1.call-done = bf16[64,2304]{1,0:T(8,128)(2,1)} async-done(((bf16[256,2304]{1,0:T(8,128)(2,1)}), bf16[64,2304]{1,0:T(8,128)(2,1)}) %reduce-scatter.4.cloned.1.call-update) | async-done | bytes 294928 | tf_op jit(solution)/shard_map/reduce_scatter | solution.py:104
  90.1 1.5 reshape.213
  91.7 34.8 %reduce-scatter.6.cloned.1.call-done = bf16[64,3072]{1,0:T(8,128)(2,1)} async-done(((bf16[256,3072]{1,0:T(8,128)(2,1)}), bf16[64,3072]{1,0:T(8,128)(2,1)}) %reduce-scatter.6.cloned.1.call-update) | async-done | bytes 393232 | tf_op jit(solution)/shard_map/reduce_scatter | solution.py:147
  126.5 3.5 %fusion.9 = bf16[64,3072]{1,0:T(8,128)(2,1)} fusion(bf16[64,3072]{1,0:T(8,128)(2,1)} %reduce-scatter.6.cloned.1.call-done), kind=kLoop, calls=%fused_computation.21 | loop fusion | flops 12976128 | bytes 786432 | tf_op jit(solution)/shard_map/convert_element_type | solution.py:153
  132.6 4.2 %collective-permute-done = bf16[1,64,768]{2,1,0:T(8,128)(2,1)S(1)} collective-permute-done((bf16[1,64,768]{2,1,0:T(8,128)(2,1)S(1)}, bf16[1,64,768]{2,1,0:T(8,128)(2,1)S(1)}, u32[]{:S(2)}, u32[]{:S(2)}) %collective-permute-start) | collective-permute-done | bytes 98336 | tf_op jit(solution)/shard_map/ppermute | solution.py:21
  136.9 1.4 collective-permute-start.1
  138.4 20.6 %collective-permute-done.1 = bf16[2,64,768]{2,1,0:T(8,128)(2,1)S(1)} collective-permute-done((bf16[2,64,768]{2,1,0:T(8,128)(2,1)S(1)}, bf16[2,64,768]{2,1,0:T(8,128)(2,1)S(1)}, u32[]{:S(2)}, u32[]{:S(2)}) %collective-permute-start.1) | collective-permute-done | bytes 196640 | tf_op jit(solution)/shard_map/ppermute | solution.py:21
  159.0 14.0 %all-gather.3.cloned.1.call-done = bf16[256,3072]{1,0:T(8,128)(2,1)} async-done(((bf16[64,3072]{1,0:T(8,128)(2,1)}), bf16[256,3072]{1,0:T(8,128)(2,1)}) %all-gather.3.cloned.1.call-update) | async-done | bytes 1572880 | tf_op jit(solution)/shard_map/all_gather | solution.py:156
  173.0 5.6 %fusion.86 = f32[256,1536]{1,0:T(8,128)S(1)} fusion(bf16[256,3072]{1,0:T(8,128)(2,1)} %all-gather.3.cloned.1.call-done, bf16[3072,1536]{1,0:T(8,128)(2,1)} %param.20), kind=kOutput, calls=%fused_computation.130 | convolution fusion | flops 2415919104 | bytes 12582912 | tf_op jit(solution)/shard_map/dot_general | solution.py:161
  178.6 1.7 fusion.2
  180.5 0.8 convert_element_type.121
  181.5 1.1 broadcast_select_fusion.3
  182.7 18.0 %all-gather = bf16[8,64,768]{2,1,0:T(8,128)(2,1)S(1)} all-gather(bf16[2,64,768]{2,1,0:T(8,128)(2,1)S(1)} %pad_maximum_fusion.2), channel_id=2, replica_groups=mesh['row'=8,'col'=4] {'col'}, dimensions={0}, use_global_device_ids=true | all-gather | bytes 983040 | tf_op jit(solution)/shard_map/all_gather | solution.py:143
  200.7 0.7 fusion.39
  201.4 0.7 copy.59
  202.1 12.8 %reduce-scatter.8.cloned.1.call-done = bf16[32,1536]{1,0:T(8,128)(2,1)} async-done(((bf16[256,1536]{1,0:T(8,128)(2,1)}), bf16[32,1536]{1,0:T(8,128)(2,1)}) %reduce-scatter.8.cloned.1.call-update) | async-done | bytes 98320 | tf_op jit(solution)/shard_map/reduce_scatter | solution.py:158
  214.9 1.6 fusion.49
  (56 shorter events, 4.2 us)
Async XLA Ops:
  7.2 37.1 %copy-start = (bf16[64,16,1536]{2,1,0:T(8,128)(2,1)S(1)}, bf16[64,16,1536]{2,1,0:T(8,128)(2,1)}, u32[]{:S(2)}) copy-start(bf16[64,16,1536]{2,1,0:T(8,128)(2,1)} %param.16) | copy-start | bytes 9437188
  7.2 83.0 %reduce-scatter.4.cloned.1.call-start = ((), (), s32[]{:S(2)}) async-start(), calls=%async_computation.3 | async-start | bytes 1474560 | tf_op jit(solution)/shard_map/reduce_scatter | solution.py:104
  45.5 10.4 %copy-start.2 = (bf16[256,1536]{1,0:T(8,128)(2,1)S(1)}, bf16[256,1536]{1,0:T(8,128)(2,1)}, u32[]{:S(2)}) copy-start(bf16[256,1536]{1,0:T(8,128)(2,1)} %all_gather.12) | copy-start | bytes 2359300
  63.5 63.0 %reduce-scatter.6.cloned.1.call-start = ((), (), s32[]{:S(2)}) async-start(), calls=%async_computation.4 | async-start | bytes 1966080 | tf_op jit(solution)/shard_map/reduce_scatter | solution.py:147
  73.9 7.5 %copy-start.5 = (s32[4]{0:T(128)S(1)}, s32[4]{0:T(128)}, u32[]{:S(2)}) copy-start(s32[4]{0:T(128)} %param.21) | copy-start | bytes 52
  81.4 91.6 %all-gather.3.cloned.1.call-start = ((), (), s32[]{:S(2)}) async-start(), calls=%async_computation.5 | async-start | bytes 1966080 | tf_op jit(solution)/shard_map/all_gather | solution.py:156
  130.0 84.9 %reduce-scatter.8.cloned.1.call-start = ((), (), s32[]{:S(2)}) async-start(), calls=%async_computation.6 | async-start | bytes 884736 | tf_op jit(solution)/shard_map/reduce_scatter | solution.py:158
  132.2 4.7 %collective-permute-start = (bf16[1,64,768]{2,1,0:T(8,128)(2,1)S(1)}, bf16[1,64,768]{2,1,0:T(8,128)(2,1)S(1)}, u32[]{:S(2)}, u32[]{:S(2)}) collective-permute-start(bf16[1,64,768]{2,1,0:T(8,128)(2,1)S(1)} %broadcast_in_dim_reshape.3), channel_id=1, source_target_pairs={{0,1},{1,0},{2,3},{3,2},{4,5},{5,4},{6,7},{7,6},{8,9},{9,8},{10,11... | collective-permute-start | bytes 294920 | tf_op jit(solution)/shard_map/ppermute | solution.py:21
  136.9 22.0 %collective-permute-start.1 = (bf16[2,64,768]{2,1,0:T(8,128)(2,1)S(1)}, bf16[2,64,768]{2,1,0:T(8,128)(2,1)S(1)}, u32[]{:S(2)}, u32[]{:S(2)}) collective-permute-start(bf16[2,64,768]{2,1,0:T(8,128)(2,1)S(1)} %pad_maximum_fusion.1), channel_id=1, source_target_pairs={{0,2},{1,3},{2,0},{3,1},{4,6},{5,7},{6,4},{7,5},{8,10},{9,11},{10,... | collective-permute-start | bytes 589832 | tf_op jit(solution)/shard_map/ppermute | solution.py:21
  159.0 19.6 %copy-start.3 = (bf16[768,1536]{1,0:T(8,128)(2,1)S(1)}, bf16[768,1536]{1,0:T(8,128)(2,1)}, u32[]{:S(2)}) copy-start(bf16[768,1536]{1,0:T(8,128)(2,1)} %param.18) | copy-start | bytes 7077892
  180.3 20.4 %copy-start.6 = (s32[4]{0:T(128)S(1)}, s32[4]{0:T(128)}, u32[]{:S(2)}) copy-start(s32[4]{0:T(128)} %param.23) | copy-start | bytes 52
  181.3 33.6 %copy-start.4 = (bf16[32,1536]{1,0:T(8,128)(2,1)S(1)}, bf16[32,1536]{1,0:T(8,128)(2,1)}, u32[]{:S(2)}) copy-start(bf16[32,1536]{1,0:T(8,128)(2,1)} %param.12) | copy-start | bytes 294916
  181.3 35.2 %copy-start.1 = (bf16[64,16,1536]{2,1,0:T(8,128)(2,1)S(1)}, bf16[64,16,1536]{2,1,0:T(8,128)(2,1)}, u32[]{:S(2)}) copy-start(bf16[64,16,1536]{2,1,0:T(8,128)(2,1)} %param.16) | copy-start | bytes 9437188
Sparse Core Ops, SparseCore 0:
  63.7 26.4 reduce-scatter.3
  92.4 34.0 reduce-scatter.5
  130.1 42.8 all-gather.2
  180.5 34.3 reduce-scatter.7
